TPU v7x, 32 devices: a whole 2x2x4 slice. The times are simulated.
32 devices in a mesh: grp: 2 (over x), res: 16 (over z, y, core).
Axes of the slice: x: 2, y: 2, z: 4, core: 2. Of those that a mesh axis runs over, the one named last changes fastest.
Arguments:
- alignment_activations: bfloat16 [128, 128, 256], P('grp', 'res'), parts along dimension 0, may hold values from -6 to 6
- projection_weight: bfloat16 [256, 64], replicated, may hold values from -0.375 to 0.375
- output_weight: bfloat16 [1024, 128], replicated, may hold values from -0.1875 to 0.1875
- output_bias: float32 [128], replicated, may hold values from -3 to 3
- pair_update_gradient: bfloat16 [256, 128, 128], P(('grp', 'res')), parts along dimension 0, may hold values from -6 to 6
- sequence_mask: int32 [128], P('grp'), parts along dimension 0, may hold values 0 or 1
- residue_mask: int32 [256], P('grp'), parts along dimension 0, may hold values 0 or 1
Outputs:
- pair_increment: bfloat16 [256, 128, 128], P(('grp', 'res')), parts along dimension 0
- alignment_gradient: bfloat16 [128, 128, 256], P('grp', 'res'), parts along dimension 0
There are 2 independent parts, one for each index of `grp`. A program takes and returns all parts, laid end to end along the dimension named above; an argument that names none is the same for every part. Nothing has to cross between parts.
All inputs are finite; a program needn't handle non-finite values.
Results may differ from a plain program's by a relative error of at most 0.007.
Values may be sent and summed in bfloat16 or wider, within the bound.
No kernel may reach another device: no remote copies, remote signals or barrier semaphores. Data moves between devices by JAX's collectives and lax.ppermute only.
A program may use at most 64 MiB of HBM per device.

v0:
```python
import jax
import jax.numpy as jnp
from jax import lax
from jax.sharding import PartitionSpec as P

eps_norm = 1e-05


def layer_norm_forward(values):
    mean_val = jnp.mean(values, axis=-1, keepdims=True)
    centered = values - mean_val
    inverse_deviation = lax.rsqrt(jnp.mean(centered * centered, axis=-1, keepdims=True) + eps_norm)
    return (centered * inverse_deviation, inverse_deviation)


def layer_norm_backward(grad_out, scaled_product, inverse_deviation):
    mean_grad = jnp.mean(grad_out, axis=-1, keepdims=True)
    mean_cross = jnp.mean(grad_out * scaled_product, axis=-1, keepdims=True)
    return inverse_deviation * (grad_out - mean_grad - scaled_product * mean_cross)


def body(
    alignment_activations,
    projection_weight,
    output_weight,
    output_bias,
    pair_update_gradient,
    sequence_mask,
    residue_mask,
):
    alignment_rows = alignment_activations.shape[0]
    local_rows = alignment_activations.shape[1]
    alignment_width = alignment_activations.shape[2]
    projected_width = projection_weight.shape[1] // 2
    pair_width = output_weight.shape[1]
    row_start = lax.axis_index("res") * local_rows
    residue_float_mask = residue_mask.astype(jnp.float32)
    local_residues = lax.dynamic_slice_in_dim(residue_float_mask, row_start, local_rows)
    alignment_mask = sequence_mask.astype(jnp.float32)[:, None] * local_residues[None, :]
    scaled_product, inverse_deviation = layer_norm_forward(
        alignment_activations.astype(jnp.float32)
    )
    normalized_input = scaled_product.astype(jnp.bfloat16)
    projected_rows = jnp.dot(
        normalized_input.reshape(-1, alignment_width),
        projection_weight,
        preferred_element_type=jnp.float32,
    )
    projected_rows = (
        projected_rows.reshape(alignment_rows, local_rows, 2 * projected_width)
        * alignment_mask[:, :, None]
    )
    projected_rows = projected_rows.astype(jnp.bfloat16)
    left_projected = projected_rows[:, :, :projected_width]
    right_proj = projected_rows[:, :, projected_width:]
    live_rows = jnp.sum(sequence_mask.astype(jnp.float32))
    right_all = lax.all_gather(right_proj, "res", axis=1, tiled=True)
    residue_count = right_all.shape[1]
    block_columns = 256 if residue_count % 256 == 0 else residue_count
    block_count = residue_count // block_columns
    count_rows = jnp.maximum(live_rows * local_residues[:, None] * residue_float_mask[None, :], 1.0)

    def pair_block(carry, block_id):
        pair_increment, left_gradient, gradient_pieces = carry
        column_offset = block_id * block_columns
        right_blk = lax.dynamic_slice_in_dim(right_all, column_offset, block_columns, 1)
        cot_blk = lax.dynamic_slice_in_dim(pair_update_gradient, column_offset, block_columns, 1)
        count_blk = lax.dynamic_slice_in_dim(count_rows, column_offset, block_columns, 1)
        outer = jnp.einsum(
            "sic,sjd->ijcd", left_projected, right_blk, preferred_element_type=jnp.float32
        )
        outer = outer.astype(jnp.bfloat16).reshape(-1, projected_width * projected_width)
        update = jnp.dot(outer, output_weight, preferred_element_type=jnp.float32)
        update = update.reshape(local_rows, block_columns, pair_width) + output_bias
        update = (update / count_blk[:, :, None]).astype(jnp.bfloat16)
        pair_increment = lax.dynamic_update_slice_in_dim(pair_increment, update, column_offset, 1)
        grad_outer = jnp.dot(
            cot_blk.reshape(-1, pair_width), output_weight.T, preferred_element_type=jnp.float32
        )
        grad_outer = (
            grad_outer.reshape(local_rows, block_columns, projected_width, projected_width)
            / count_blk[:, :, None, None]
        )
        grad_outer = grad_outer.astype(jnp.bfloat16)
        left_gradient = left_gradient + jnp.einsum(
            "ijcd,sjd->sic", grad_outer, right_blk, preferred_element_type=jnp.float32
        )
        gradient_piece = jnp.einsum(
            "ijcd,sic->jsd", grad_outer, left_projected, preferred_element_type=jnp.float32
        )
        gradient_pieces = lax.dynamic_update_slice_in_dim(
            gradient_pieces,
            gradient_piece.reshape(block_columns, alignment_rows * projected_width),
            column_offset,
            0,
        )
        return ((pair_increment, left_gradient, gradient_pieces), None)

    start_update = jnp.zeros((local_rows, residue_count, pair_width), jnp.bfloat16)
    initial_left = jnp.zeros((alignment_rows, local_rows, projected_width), jnp.float32)
    initial_pieces = jnp.zeros((residue_count, alignment_rows * projected_width), jnp.float32)
    (pair_increment, left_gradient, gradient_pieces), unused = lax.scan(
        pair_block, (start_update, initial_left, initial_pieces), jnp.arange(block_count)
    )
    gradient_total = lax.psum_scatter(gradient_pieces, "res", scatter_dimension=0, tiled=True)
    right_gradient = gradient_total.reshape(local_rows, alignment_rows, projected_width).transpose(
        1, 0, 2
    )
    projection_gradient = (
        jnp.concatenate([left_gradient, right_gradient], axis=-1) * alignment_mask[:, :, None]
    )
    projection_gradient = projection_gradient.astype(jnp.bfloat16)
    normalized_gradient = jnp.dot(
        projection_gradient.reshape(-1, 2 * projected_width),
        projection_weight.T,
        preferred_element_type=jnp.float32,
    )
    normalized_gradient = normalized_gradient.reshape(alignment_rows, local_rows, alignment_width)
    alignment_gradient = layer_norm_backward(
        normalized_gradient, scaled_product, inverse_deviation
    ).astype(jnp.bfloat16)
    return (pair_increment, alignment_gradient)


def solution(mesh):
    in_specs = (
        P("grp", "res", None),
        P(),
        P(),
        P(),
        P(("grp", "res"), None, None),
        P("grp"),
        P("grp"),
    )
    out_specs = (P(("grp", "res"), None, None), P("grp", "res", None))
    return jax.shard_map(body, mesh=mesh, in_specs=in_specs, out_specs=out_specs, check_vma=False)
```

profile of v0, /device:TPU:0, one launch (start us, length us, event | category | flops | bytes accessed | tf_op | source)
XLA Modules:
  0.0 89.6 jit_solution(17013610262894951195)
XLA Ops:
  7.2 0.0 copy-start
  7.2 0.0 copy-start.7
  7.2 0.0 reduce-scatter.4.cloned.1.call-start
  7.2 1.3 %convert_reduce_fusion.1 = f32[]{:T(128)} fusion(s32[64]{0:T(128)} %param.12), kind=kLoop, calls=%fused_computation.46 | loop fusion | flops 127 | bytes 260 | tf_op jit(solution)/shard_map/reduce_sum | solution.py:56
  8.5 0.7 convert_element_type.41
  9.2 0.7 convert_element_type.42
  9.9 1.1 %convert_reduce_fusion = f32[64,8]{1,0:T(8,128)S(1)} fusion(bf16[64,8,256]{2,1,0:T(8,128)(2,1)} %param.7), kind=kLoop, calls=%fused_computation.15 | loop fusion | flops 261632 | bytes 264192 | tf_op jit(solution)/shard_map/reduce_sum | solution.py:10
  11.0 1.2 %fusion.23 = f32[64,8]{1,0:T(8,128)S(1)} fusion(bf16[64,8,256]{2,1,0:T(8,128)(2,1)} %param.7, f32[64,8]{1,0:T(8,128)S(1)} %broadcast_multiply_fusion.3), kind=kLoop, calls=%fused_computation.25 | loop fusion | flops 523776 | bytes 266240 | tf_op jit(solution)/shard_map/reduce_sum | solution.py:12
  12.2 0.7 broadcast_multiply_fusion.4
  12.9 0.1 add_rsqrt_fusion
  13.0 0.0 copy-start.4
  13.0 0.6 copy-done.4
  13.6 1.3 %fusion.9 = bf16[64,8,64]{2,1,0:T(8,128)(2,1)S(1)} fusion(bf16[64,8,256]{2,1,0:T(8,128)(2,1)} %param.7, f32[64,8]{1,0:T(8,128)S(1)} %get-tuple-element.29, f32[64,8]{1,0:T(8,128)S(1)} %broadcast_multiply_fusion.3, f32[64,8]{1,0:T(8,128)S(1)} %get-tuple-element.40, bf16[256,64]{0,1:T(8,128)(2,1)} %param.8), kind=kOutput, calls=%fused_computation.11 | convolution fusion | flops 17367040 | bytes 366592 | tf_op jit(solution)/shard_map/dot_general | solution.py:44
  14.8 0.1 fusion.39
  14.9 0.1 copy.23
  15.1 0.1 multiply_maximum_fusion
  15.2 0.0 copy-done
  15.2 0.0 copy-done.7
  15.2 0.7 divide_convert_fusion
  15.9 0.0 copy-start.2
  15.9 0.8 fusion.4
  16.7 0.6 copy.30
  17.3 0.0 copy-done.2
  17.3 1.3 %copy.43 = f32[128,2048]{1,0:T(8,128)} copy(f32[128,2048]{0,1:T(8,128)S(1)} %bitcast.49) | data formatting | bytes 2097152
  18.6 0.0 reduce-scatter.4.cloned.1.call-update
  18.7 32.3 %all_gather.3 = bf16[64,128,32]{2,1,0:T(8,128)(2,1)S(1)} all-gather(bf16[64,8,32]{2,1,0:T(8,128)(2,1)S(1)} %get-tuple-element.27), channel_id=1, replica_groups=mesh['grp'=2,'res'=16] {'res'}, dimensions={1}, use_global_device_ids=true | all-gather | bytes 557056 | tf_op jit(solution)/shard_map/all_gather | solution.py:57
  51.0 3.2 %copy.26 = bf16[64,128,32]{0,1,2:T(8,128)(2,1)S(1)} copy(bf16[64,128,32]{2,1,0:T(8,128)(2,1)S(1)} %all_gather.3) | data formatting | bytes 1048576 | tf_op jit(solution)/shard_map/all_gather | solution.py:57
  54.1 3.0 %fusion.10 = f32[64,8,32]{0,2,1:T(8,128)} fusion(bf16[8,128,32,32]{1,3,2,0:T(8,128)(2,1)} %copy-done.2, bf16[64,128,32]{0,1,2:T(8,128)(2,1)S(1)} %copy.26), kind=kOutput, calls=%fused_computation.12 | convolution fusion | flops 134217728 | bytes 2686976 | tf_op jit(solution)/shard_map/while/body/eval_jaxpr/ijcd,sjd->sic/dot_general | solution.py:85
  57.1 1.7 %copy.33 = f32[64,8,32]{2,1,0:T(8,128)} copy(f32[64,8,32]{0,2,1:T(8,128)} %fusion.10) | data formatting | bytes 131072 | tf_op jit(solution)/shard_map/while/body/eval_jaxpr/ijcd,sjd->sic/dot_general | solution.py:85
  58.9 3.2 %copy.34 = bf16[64,128,32,1]{0,1,3,2:T(8,128)(2,1)S(1)} copy(bf16[64,128,32,1]{2,1,0,3:T(8,128)(2,1)S(1)} %bitcast.47) | data formatting | bytes 1048576 | tf_op jit(solution)/shard_map/all_gather | solution.py:57
  62.1 0.7 convert_bitcast_fusion
  62.8 0.0 copy-start.8
  62.8 1.4 %copy.24 = bf16[8,128,32,32]{1,3,2,0:T(8,128)(2,1)S(1)} copy(bf16[8,128,32,32]{1,2,0,3:T(8,128)(2,1)S(1)} %convert_bitcast_fusion) | data formatting | bytes 4194304 | tf_op jit(solution)/shard_map/while/body/eval_jaxpr/convert_element_type | solution.py:72
  64.1 0.0 copy-done.8
  64.2 1.5 %fusion.8 = bf16[8,128,128]{2,1,0:T(8,128)(2,1)} fusion(bf16[8,128,1024]{1,2,0:T(8,128)(2,1)S(1)} %bitcast.50, bf16[1024,128]{1,0:T(8,128)(2,1)S(1)} %copy-done, f32[8,128]{1,0:T(8,128)S(1)} %multiply_maximum_fusion, f32[128]{0:T(128)S(1)} %copy-done.8), kind=kOutput, calls=%fused_computation.9 | convolution fusion | flops 268828672 | bytes 2626048 | tf_op jit(solution)/shard_map/while/body/eval_jaxpr/dot_general | solution.py:73
  65.6 0.0 copy-start.1
  65.7 0.0 copy-start.3
  65.7 0.0 copy-start.5
  65.7 0.0 copy-start.6
  65.7 14.0 %reduce-scatter.4.cloned.1.call-done = f32[8,2048]{1,0:T(8,128)} async-done(((f32[128,2048]{1,0:T(8,128)}), f32[8,2048]{1,0:T(8,128)}) %reduce-scatter.4.cloned.1.call-update) | async-done | bytes 65552
  79.7 1.2 %copy.44 = f32[8,2048]{0,1:T(8,128)S(1)} copy(f32[8,2048]{1,0:T(8,128)} %reduce-scatter.4.cloned.1.call-done) | data formatting | bytes 131072
  80.9 0.3 copy.32
  81.2 0.0 copy-done.1
  81.2 0.0 copy-done.3
  81.2 0.0 copy-done.5
  81.2 0.0 copy-done.6
  81.2 0.5 fusion.38
  81.8 1.0 %fusion.22 = bf16[64,8,256]{2,1,0:T(8,128)(2,1)} fusion(bf16[64,8,256]{2,1,0:T(8,128)(2,1)S(1)} %copy-done.1, f32[64,8,256]{2,1,0:T(8,128)S(1)} %get-tuple-element.28, f32[64,8]{1,0:T(8,128)S(1)} %broadcast_multiply_fusion.1, f32[64,8]{1,0:T(8,128)S(1)} %broadcast_multiply_fusion.2, f32[64,8]{1,0:T(8,128)S(1)} %get-tuple-element.29, ...), kind=kLoop, calls=%fused_computation.24 | loop fusion | flops 1048576 | bytes 1056768 | tf_op jit(solution)/shard_map/convert_element_type | solution.py:121
  (3 shorter events, 0.0 us)
Async XLA Ops:
  7.2 8.0 %copy-start = (bf16[1024,128]{1,0:T(8,128)(2,1)S(1)}, bf16[1024,128]{1,0:T(8,128)(2,1)}, u32[]{:S(2)}) copy-start(bf16[1024,128]{1,0:T(8,128)(2,1)} %param.9) | copy-start | bytes 786436
  7.2 8.0 %copy-start.7 = (bf16[8,128,128]{2,1,0:T(8,128)(2,1)S(1)}, bf16[8,128,128]{2,1,0:T(8,128)(2,1)}, u32[]{:S(2)}) copy-start(bf16[8,128,128]{2,1,0:T(8,128)(2,1)} %param.11) | copy-start | bytes 786436
  7.2 72.5 %reduce-scatter.4.cloned.1.call-start = ((), (), s32[]{:S(2)}) async-start(), calls=%async_computation.1 | async-start | bytes 1114112
  13.0 0.6 copy-start.4
  15.9 1.4 %copy-start.2 = (bf16[8,128,32,32]{1,3,2,0:T(8,128)(2,1)}, bf16[8,128,32,32]{1,3,2,0:T(8,128)(2,1)S(1)}, u32[]{:S(2)}) copy-start(bf16[8,128,32,32]{1,3,2,0:T(8,128)(2,1)S(1)} %divide_convert_fusion) | copy-start | bytes 6291460
  62.8 1.4 %copy-start.8 = (f32[128]{0:T(128)S(1)}, f32[128]{0:T(128)}, u32[]{:S(2)}) copy-start(f32[128]{0:T(128)} %param.10) | copy-start | bytes 1540
  65.6 15.5 %copy-start.1 = (bf16[64,8,256]{2,1,0:T(8,128)(2,1)S(1)}, bf16[64,8,256]{2,1,0:T(8,128)(2,1)}, u32[]{:S(2)}) copy-start(bf16[64,8,256]{2,1,0:T(8,128)(2,1)} %param.7) | copy-start | bytes 786436
  65.7 15.5 %copy-start.3 = (f32[64,8,32]{2,1,0:T(8,128)S(1)}, f32[64,8,32]{2,1,0:T(8,128)}, u32[]{:S(2)}) copy-start(f32[64,8,32]{2,1,0:T(8,128)} %copy.33) | copy-start | bytes 196612
  65.7 15.5 %copy-start.5 = (f32[64,8]{1,0:T(8,128)S(1)}, f32[64,8]{1,0:T(8,128)}, u32[]{:S(2)}) copy-start(f32[64,8]{1,0:T(8,128)} %copy-done.4) | copy-start | bytes 6148
  65.7 15.6 %copy-start.6 = (bf16[256,64]{0,1:T(8,128)(2,1)S(1)}, bf16[256,64]{0,1:T(8,128)(2,1)}, u32[]{:S(2)}) copy-start(bf16[256,64]{0,1:T(8,128)(2,1)} %param.8) | copy-start | bytes 98308
Sparse Core Ops, SparseCore 0:
  18.8 60.8 reduce-scatter.3
where the time goes:
time: 90 us; the launch traced here: 89.6 us
  blocking collectives  32.3 us (36%)
  between operations  14.2 us (16%)
  waiting for transfers between devices  14 us (16%)
  local copies, waits for them, and re-layouts  13.8 us (15%)
  matrix products  8.48 us (9%)
  other arithmetic  6.82 us (8%)
    all_gather x1, blocking collectives, body(): right_all = lax.all_gather(right_proj, 'res', axis=1, tiled=True)  32.3 us
    unnamed x2, waiting for transfers between devices  14 us
    all_gather x2, local copies, waits for them, and re-layouts, body(): right_all = lax.all_gather(right_proj, 'res', axis=1, tiled=True)  6.35 us
    unnamed x20, local copies, waits for them, and re-layouts  3.13 us
    dot_general x1, matrix products, pair_block(): jnp.einsum('ijcd,sjd->sic', grad_outer, right_blk, preferred_element_type...  2.99 us
  transfers between devices with their start and end apart: 1, of which 1 were waited for; matrix products, arithmetic and copies ran while one was open for 16% of the time, Pallas kernels for 0%

commit v1 on v0

v1 whole, which is shorter than its diff:
```python
import functools

import jax
import jax.numpy as jnp
from jax import lax
from jax.experimental import pallas as pl
from jax.experimental.pallas import tpu as pltpu
from jax.sharding import PartitionSpec as P

eps_norm = 1e-05
F32, BF16 = jnp.float32, jnp.bfloat16
LANES = 128
NT = (((1,), (1,)), ((), ()))
TN = (((0,), (0,)), ((), ()))


def dot(a, b, dims=(((1,), (0,)), ((), ()))):
    return lax.dot_general(a, b, dims, preferred_element_type=F32)


def exchange_masks(size):
    return [1 << k for k in range(size.bit_length() - 1)]


def block_masks(size):
    masks = exchange_masks(size)
    order = []
    for m in range(size):
        mask = 0
        for k, b in enumerate(masks):
            if (m >> (len(masks) - 1 - k)) & 1:
                mask ^= b
        order.append(mask)
    return order


def pack_mask(seq_ref, residue_of, count):
    seqs = seq_ref.shape[1]
    per = LANES // seqs
    seq = jnp.concatenate([seq_ref[...].astype(F32)] * per, axis=1)
    lane = lax.broadcasted_iota(jnp.int32, (1, LANES), 1)
    tiles = []
    for q in range(count // per):
        live = jnp.zeros((1, LANES), F32)
        for k in range(per):
            here = (lane >= k * seqs) & (lane < (k + 1) * seqs)
            live = jnp.where(here, residue_of(q * per + k), live)
        tiles.append(seq * live)
    return tiles


def project_kernel(x_ref, w_ref, seq_ref, res_ref, rloc_ref, left_ref, scaled_ref, inv_ref, rows, invs, zs):
    seqs, local, width = x_ref.shape
    chans = w_ref.shape[0] // 2
    half = chans // 2
    me = lax.axis_index("res")
    x = x_ref[...].astype(F32).reshape(seqs * local, width)
    cen = x - jnp.mean(x, axis=-1, keepdims=True)
    inv = lax.rsqrt(jnp.mean(cen * cen, axis=-1, keepdims=True) + eps_norm)
    scaled = cen * inv
    for h in range(width // LANES):
        rows[h] = scaled[:, h * LANES : (h + 1) * LANES]
    invs[...] = jnp.broadcast_to(inv, invs.shape)
    for j in range(local):
        for h in range(width // LANES):
            scaled_ref[j * seqs : (j + 1) * seqs, h * LANES : (h + 1) * LANES] = rows[
                h, pl.ds(j, seqs, stride=local), :
            ]
        inv_ref[j * seqs : (j + 1) * seqs, :] = invs[pl.ds(j, seqs, stride=local), :]
    pt = dot(w_ref[...], scaled_ref[...].astype(BF16), NT)
    mask = pack_mask(seq_ref, lambda j: res_ref[me * local + j].astype(F32), local)
    pt = pt * jnp.concatenate(mask, axis=1)
    left_ref[...] = pt[:chans].T.astype(BF16)
    lane = lax.broadcasted_iota(jnp.int32, (half, LANES), 1)
    for q in range(local // 2):
        lo = pt[chans : chans + half, q * LANES : (q + 1) * LANES]
        hi = pt[chans + half :, q * LANES : (q + 1) * LANES]
        zs[2 * q * half : (2 * q + 1) * half, :] = jnp.where(lane < seqs, lo, pltpu.roll(hi, seqs, 1))
        zs[(2 * q + 1) * half : (2 * q + 2) * half, :] = jnp.where(lane < seqs, pltpu.roll(lo, seqs, 1), hi)
    for dd in range(half):
        rloc_ref[:, dd * LANES : (dd + 1) * LANES] = zs[pl.ds(dd, local, stride=half), :].astype(BF16)


def pull_kernel(order, left_ref, wo_ref, g_ref, lp_ref, keep_ref, send_ref, grel_ref, wd_ref, w32, g32):
    local, total, pair = g_ref.shape
    chans = left_ref.shape[1]
    seqs = left_ref.shape[0] // local
    half = chans // 2
    me = lax.axis_index("res")
    w32[...] = wo_ref[...].astype(F32)
    for d in range(chans):
        wd_ref[d * chans : (d + 1) * chans, :] = w32[pl.ds(d, chans, stride=chans), :].astype(BF16)
    g32[...] = g_ref[...].astype(F32)
    for m in range(0, len(order), 2):
        one = pl.multiple_of((me ^ order[m]) * local, local)
        two = pl.multiple_of((me ^ order[m + 1]) * local, local)
        for i in range(local):
            block = jnp.concatenate([g32[i, pl.ds(one, local), :], g32[i, pl.ds(two, local), :]], axis=0)
            grel_ref[m * local : (m + 2) * local, i * pair : (i + 1) * pair] = block.astype(BF16)
    left = left_ref[...]
    mid = total // 2
    for dd in range(0, half, 2):
        for k in (dd, dd + 1):
            w = jnp.concatenate(
                [wd_ref[k * chans : (k + 1) * chans, :], wd_ref[(k + half) * chans : (k + half + 1) * chans, :]],
                axis=1,
            )
            x = dot(left, w).astype(BF16)
            for i in range(local):
                for h in range(2):
                    lp_ref[k * LANES + h * seqs : k * LANES + (h + 1) * seqs, i * pair : (i + 1) * pair] = x[
                        i * seqs : (i + 1) * seqs, h * pair : (h + 1) * pair
                    ]
        cols = slice(dd * LANES, (dd + 2) * LANES)
        part = dot(grel_ref[...], lp_ref[cols, :], NT)
        keep_ref[:, cols] = part[:mid]
        send_ref[:, cols] = part[mid:].astype(BF16)


def relative_row(row, order, me, local, col, rel):
    total = row.shape[1]
    col[...] = jnp.broadcast_to(row, (LANES, total)).T
    for m, mask in enumerate(order):
        rel[m * local : (m + 1) * local, :] = col[pl.ds(pl.multiple_of((me ^ mask) * local, local), local), :]
    return rel[...].T[:1, :]


def outer_grad_kernel(order, wd_ref, grel_ref, seq_ref, res_ref, ress_ref, got_ref, col, rel):
    total = grel_ref.shape[0]
    pair = wd_ref.shape[1]
    local = grel_ref.shape[1] // pair
    chans = got_ref.shape[0] // (2 * local)
    half = chans // 2
    me = lax.axis_index("res")
    live = jnp.sum(seq_ref[...].astype(F32))
    live_row = relative_row(res_ref[...].astype(F32), order, me, local, col, rel) * live
    for i in range(local):
        count = jnp.maximum(live_row * ress_ref[me * local + i].astype(F32), 1.0)
        t = dot(wd_ref[...], grel_ref[:, i * pair : (i + 1) * pair], NT) * (1.0 / count)
        t = t.astype(BF16)
        for d in range(chans):
            h, dd = divmod(d, half)
            got_ref[(h * local + i) * chans : (h * local + i + 1) * chans, dd * total : (dd + 1) * total] = t[
                d * chans : (d + 1) * chans, :
            ]


def pair_kernel(order, r_ref, lp_ref, got_ref, bias_ref, seq_ref, res_ref, ress_ref, pair_ref, gl_ref, ubuf):
    local, total, pair = pair_ref.shape
    half = r_ref.shape[1] // LANES
    me = lax.axis_index("res")
    live = jnp.sum(seq_ref[...].astype(F32))
    acc = None
    for dd in range(0, half, 2):
        rows = jnp.concatenate(
            [r_ref[:, dd * LANES : (dd + 1) * LANES], r_ref[:, (dd + 1) * LANES : (dd + 2) * LANES]], axis=0
        )
        t = dot(got_ref[:, dd * total : (dd + 2) * total], rows)
        acc = t if acc is None else acc + t
    gl_ref[...] = acc
    live_col = jnp.broadcast_to(res_ref[...].astype(F32) * live, (LANES, total)).T
    bias = bias_ref[...]
    for i in range(0, local, 2):
        u = dot(r_ref[...], lp_ref[:, i * pair : (i + 2) * pair])
        for m, mask in enumerate(order):
            ubuf[pl.ds(pl.multiple_of((me ^ mask) * local, local), local), :] = u[m * local : (m + 1) * local, :]
        for k in range(2):
            count = jnp.maximum(live_col * ress_ref[me * local + i + k].astype(F32), 1.0)
            pair_ref[i + k] = ((ubuf[:, k * pair : (k + 1) * pair] + bias) * (1.0 / count)).astype(BF16)


def final_kernel(gl_ref, gr_ref, scaled_ref, inv_ref, w_ref, seq_ref, res_ref, out_ref, zs, proj, rows):
    seqs, local, width = out_ref.shape
    chans = w_ref.shape[0] // 2
    half = chans // 2
    me = lax.axis_index("res")
    live = jnp.sum(seq_ref[...].astype(F32))
    for dd in range(half):
        zs[pl.ds(dd, local, stride=half), :] = gr_ref[:, dd * LANES : (dd + 1) * LANES]

    def scale_of(j):
        keep = res_ref[me * local + j].astype(F32)
        return keep / jnp.maximum(live * keep, 1.0)

    mask = pack_mask(seq_ref, lambda j: res_ref[me * local + j].astype(F32), local)
    scale = pack_mask(seq_ref, scale_of, local)
    lane_c = lax.broadcasted_iota(jnp.int32, (chans, LANES), 1) < seqs
    lane_h = lax.broadcasted_iota(jnp.int32, (half, LANES), 1) < seqs
    for q in range(local // 2):
        cols = slice(q * LANES, (q + 1) * LANES)
        a, b = 2 * q, 2 * q + 1
        lo_a = gl_ref[a * chans : (a + 1) * chans, :]
        hi_a = gl_ref[(local + a) * chans : (local + a + 1) * chans, :]
        lo_b = gl_ref[b * chans : (b + 1) * chans, :]
        hi_b = gl_ref[(local + b) * chans : (local + b + 1) * chans, :]
        left = jnp.where(lane_c, lo_a + pltpu.roll(hi_a, seqs, 1), pltpu.roll(lo_b, seqs, 1) + hi_b)
        proj[:chans, cols] = (left * mask[q]).astype(BF16)
        za = zs[a * half : (a + 1) * half, :]
        zb = zs[b * half : (b + 1) * half, :]
        low = jnp.where(lane_h, za, pltpu.roll(zb, seqs, 1))
        high = jnp.where(lane_h, pltpu.roll(za, seqs, 1), zb)
        proj[chans : chans + half, cols] = (low * scale[q]).astype(BF16)
        proj[chans + half :, cols] = (high * scale[q]).astype(BF16)
    grad = dot(proj[...], w_ref[...], TN)
    scaled = scaled_ref[...]
    inv = inv_ref[:, :1]
    mean_grad = jnp.mean(grad, axis=-1, keepdims=True)
    mean_cross = jnp.mean(grad * scaled, axis=-1, keepdims=True)
    res = inv * (grad - mean_grad - scaled * mean_cross)
    for j in range(local):
        for h in range(width // LANES):
            rows[h, pl.ds(j, seqs, stride=local), :] = res[
                j * seqs : (j + 1) * seqs, h * LANES : (h + 1) * LANES
            ]
    for h in range(width // LANES):
        out_ref[:, :, h * LANES : (h + 1) * LANES] = rows[h].reshape(seqs, local, LANES).astype(BF16)


def shape(dims, dtype):
    return jax.ShapeDtypeStruct(dims, dtype)


VM = pl.BlockSpec(memory_space=pltpu.VMEM)
SM = pl.BlockSpec(memory_space=pltpu.SMEM)


def body(size, acts, proj_w, out_w, out_b, cot, seq_mask, res_mask):
    seqs, local, width = acts.shape
    chans = proj_w.shape[1] // 2
    pair = out_w.shape[1]
    total = cot.shape[1]
    flat = chans * seqs
    half = chans // 2
    order = block_masks(size)
    masks = exchange_masks(size)
    proj_t = proj_w.T
    seq_row = seq_mask.reshape(1, seqs)
    res_row = res_mask.reshape(1, total)

    r, left, scaled, inv = pl.pallas_call(
        project_kernel,
        out_shape=(
            shape((local, flat), BF16),
            shape((local * seqs, chans), BF16),
            shape((local * seqs, width), F32),
            shape((local * seqs, LANES), F32),
        ),
        in_specs=[VM, VM, VM, SM],
        out_specs=(VM, VM, VM, VM),
        scratch_shapes=[
            pltpu.VMEM((width // LANES, seqs * local, LANES), F32),
            pltpu.VMEM((seqs * local, LANES), F32),
            pltpu.VMEM((local * half, LANES), F32),
        ],
        name="project",
    )(acts, proj_t, seq_row, res_mask)

    lp, keep, send, grel, wd = pl.pallas_call(
        functools.partial(pull_kernel, order),
        out_shape=(
            shape((flat, local * pair), BF16),
            shape((total // 2, flat), F32),
            shape((total // 2, flat), BF16),
            shape((total, local * pair), BF16),
            shape(out_w.shape, BF16),
        ),
        in_specs=[VM] * 3,
        out_specs=(VM,) * 5,
        scratch_shapes=[pltpu.VMEM(out_w.shape, F32), pltpu.VMEM(cot.shape, F32)],
        name="pull",
    )(left, out_w, cot)

    got = pl.pallas_call(
        functools.partial(outer_grad_kernel, order),
        out_shape=shape((2 * local * chans, half * total), BF16),
        in_specs=[VM, VM, VM, VM, SM],
        out_specs=VM,
        scratch_shapes=[pltpu.VMEM((total, LANES), F32), pltpu.VMEM((total, LANES), F32)],
        name="outer_grad",
    )(wd, grel, seq_row, res_row, res_mask)

    def swap(v, b):
        return lax.ppermute(v, "res", [(i, i ^ b) for i in range(size)])

    for b in reversed(masks):
        r = jnp.concatenate([r, swap(r, b)], axis=0)

    right = keep + swap(send, masks[0]).astype(F32)
    for b in masks[1:]:
        h = right.shape[0] // 2
        right = right[:h] + swap(right[h:].astype(BF16), b).astype(F32)

    pair_out, gl = pl.pallas_call(
        functools.partial(pair_kernel, order),
        out_shape=(shape((local, total, pair), BF16), shape((2 * local * chans, LANES), F32)),
        in_specs=[VM, VM, VM, VM, VM, VM, SM],
        out_specs=(VM, VM),
        scratch_shapes=[pltpu.VMEM((total, 2 * pair), F32)],
        name="pair",
    )(r, lp, got, out_b.reshape(1, pair), seq_row, res_row, res_mask)

    grad = pl.pallas_call(
        final_kernel,
        out_shape=shape(acts.shape, BF16),
        in_specs=[VM, VM, VM, VM, VM, VM, SM],
        out_specs=VM,
        scratch_shapes=[
            pltpu.VMEM((local * half, LANES), F32),
            pltpu.VMEM((2 * chans, local * seqs), BF16),
            pltpu.VMEM((width // LANES, seqs * local, LANES), F32),
        ],
        name="final",
    )(gl, right, scaled, inv, proj_t, seq_row, res_mask)
    return pair_out, grad


def solution(mesh):
    in_specs = (
        P("grp", "res", None),
        P(),
        P(),
        P(),
        P(("grp", "res"), None, None),
        P("grp"),
        P("grp"),
    )
    out_specs = (P(("grp", "res"), None, None), P("grp", "res", None))
    return jax.shard_map(
        functools.partial(body, mesh.shape["res"]),
        mesh=mesh,
        in_specs=in_specs,
        out_specs=out_specs,
        check_vma=False,
    )
```

time: 90 us -> 49.9 us (0.55)
  blocking collectives: 32.3 us -> 0 us
  Pallas kernels: 0 us -> 19.3 us
  between operations: 14.2 us -> 0.71 us
  local copies, waits for them, and re-layouts: 13.8 us -> 1.61 us
  starting transfers between devices: 0.04 us -> 9.92 us
  matrix products: 8.48 us -> 0 us
  other arithmetic: 6.82 us -> 3.32 us
    all_gather x1 -> x0, blocking collectives: 32.3 us -> none  [body(): right_all = lax.all_gather(right_proj, 'res', axis=1, tiled=True)]
    pallas_call x0 -> x5, Pallas kernels: none -> 19.3 us  [the longest x1 5.96 us: body(): pl.pallas_call(functools.partial(pull_kernel, order), out_shape=(shape((f...]
    ppermute x0 -> x8, waiting for transfers between devices: none -> 14.6 us  [swap(): return lax.ppermute(v, 'res', [(i, i ^ b) for i in range(size)])]
    unnamed x2 -> x0, waiting for transfers between devices: 14 us -> none
    ppermute x0 -> x8, starting transfers between devices: none -> 9.92 us  [swap(): return lax.ppermute(v, 'res', [(i, i ^ b) for i in range(size)])]
    dot_general x7 -> x0, matrix products: 8.48 us -> none  [the longest x1 2.99 us: pair_block(): jnp.einsum('ijcd,sjd->sic', grad_outer, right_blk, preferred_element_type...]
    all_gather x2 -> x0, local copies, waits for them, and re-layouts: 6.35 us -> none  [body(): right_all = lax.all_gather(right_proj, 'res', axis=1, tiled=True)]
    reduce_sum x3 -> x0, other arithmetic: 3.57 us -> none  [the longest x1 1.31 us: body(): live_rows = jnp.sum(sequence_mask.astype(jnp.float32))]
  transfers between devices with their start and end apart: 1 -> 8, of which waited for: 1 -> 4; matrix products, arithmetic and copies ran while one was open for 16% -> 8% of each run, Pallas kernels for 0% -> 18%
where the time goes in v1:
time: 49.9 us; the launch traced here: 49.5 us
  Pallas kernels  19.3 us (39%)
  waiting for transfers between devices  14.6 us (29%)
  starting transfers between devices  9.92 us (20%)
  other arithmetic  3.32 us (7%)
  local copies, waits for them, and re-layouts  1.61 us (3%)
  between operations  0.71 us (1%)
    ppermute x8, waiting for transfers between devices, swap(): return lax.ppermute(v, 'res', [(i, i ^ b) for i in range(size)])  14.6 us
    ppermute x8, starting transfers between devices, swap(): return lax.ppermute(v, 'res', [(i, i ^ b) for i in range(size)])  9.92 us
    pallas_call x1, Pallas kernels, body(): pl.pallas_call(functools.partial(pull_kernel, order), out_shape=(shape((f...  5.96 us
    pallas_call x1, Pallas kernels, body(): pl.pallas_call(functools.partial(pair_kernel, order), out_shape=(shape((l...  5.14 us
    pallas_call x1, Pallas kernels, body(): pl.pallas_call(functools.partial(outer_grad_kernel, order), out_shape=sha...  3.14 us
    pallas_call x1, Pallas kernels, body(): pl.pallas_call(final_kernel, out_shape=shape(acts.shape, BF16), in_specs=...  2.6 us
    pallas_call x1, Pallas kernels, body(): pl.pallas_call(project_kernel, out_shape=(shape((local, flat), BF16), sha...  2.45 us
    unnamed x8, local copies, waits for them, and re-layouts  1.56 us
  transfers between devices with their start and end apart: 8, of which 4 were waited for; matrix products, arithmetic and copies ran while one was open for 8% of the time, Pallas kernels for 18%

profile of v1, /device:TPU:0, one launch (start us, length us, event | category | flops | bytes accessed | tf_op | source)
XLA Modules:
  0.0 49.5 jit_solution(8297254881786738311)
XLA Ops:
  0.6 2.5 %project.1 = (bf16[8,2048]{1,0:T(8,128)(2,1)}, bf16[512,32]{1,0:T(8,128)(2,1)}, f32[512,256]{1,0:T(8,128)}, f32[512,128]{1,0:T(8,128)}) custom-call(bf16[64,8,256]{2,1,0:T(8,128)(2,1)} %x_ref.1, bf16[64,256]{1,0:T(8,128)(2,1)} %bitcast.4, s32[1,64]{1,0:T(1,128)} %bitcast.8, s32[128]{0:T(128)} %res_ref.3), custom_call_target="tpu_custom_call" | custom-call | tf_op jit(solution)/shard_map/project/pallas_call | solution.py:240
  3.1 0.0 copy-start.1
  3.1 4.1 %collective-permute-start = (bf16[8,2048]{1,0:T(8,128)(2,1)}, bf16[8,2048]{1,0:T(8,128)(2,1)S(1)}, u32[]{:S(2)}, u32[]{:S(2)}) collective-permute-start(bf16[8,2048]{1,0:T(8,128)(2,1)} %get-tuple-element.13), channel_id=1, source_target_pairs={{0,8},{1,9},{2,10},{3,11},{4,12},{5,13},{6,14},{7,15},{8,0},{9,1},... | collective-permute-start | bytes 98312 | tf_op jit(solution)/shard_map/ppermute | solution.py:283
  7.1 6.0 %pull.1 = (bf16[2048,1024]{1,0:T(8,128)(2,1)}, f32[64,2048]{1,0:T(8,128)}, bf16[64,2048]{1,0:T(8,128)(2,1)}, bf16[128,1024]{1,0:T(8,128)(2,1)}, bf16[1024,128]{1,0:T(8,128)(2,1)}) custom-call(bf16[512,32]{1,0:T(8,128)(2,1)} %get-tuple-element.14.left_ref, bf16[1024,128]{1,0:T(8,128)(2,1)} %wo_ref.1, bf16[8,128,128]{2,1,0:T(8,128)(2,1)} %g_ref.1), custom_call_target="tpu_custom_call" | custom-call | tf_op jit(solution)/shard_map/pull/pallas_call | solution.py:258
  13.1 0.0 collective-permute-start.4
  13.1 0.8 %constant_dynamic-update-slice_fusion.4 = bf16[128,2048]{1,0:T(8,128)(2,1)S(1)} fusion(bf16[8,2048]{1,0:T(8,128)(2,1)} %get-tuple-element.13), kind=kLoop, calls=%fused_computation.14 | loop fusion | bytes 65536
  13.9 3.1 %outer_grad.1.got_ref = bf16[512,2048]{1,0:T(8,128)(2,1)} custom-call(bf16[1024,128]{1,0:T(8,128)(2,1)} %get-tuple-element.16.wd_ref, bf16[128,1024]{1,0:T(8,128)(2,1)} %get-tuple-element.17.grel_ref, s32[1,64]{1,0:T(1,128)} %bitcast.9, s32[1,128]{1,0:T(1,128)} %bitcast.6, s32[128]{0:T(128)} %res_ref.3), custom_call_target="tpu_custom_call" | custom-call | tf_op jit(solution)/shard_map/outer_grad/pallas_call | solution.py:273
  17.0 0.0 collective-permute-done
  17.0 0.8 %pad_maximum_fusion.2 = bf16[16,2048]{1,0:T(8,128)(2,1)S(1)} fusion(bf16[8,2048]{1,0:T(8,128)(2,1)S(1)} %collective-permute-done, bf16[8,2048]{1,0:T(8,128)(2,1)} %get-tuple-element.13), kind=kLoop, calls=%fused_computation.9 | loop fusion | flops 131072 | bytes 131072 | tf_op jit(solution)/shard_map/concatenate | solution.py:286
  17.8 1.6 %collective-permute-start.1 = (bf16[16,2048]{1,0:T(8,128)(2,1)S(1)}, bf16[16,2048]{1,0:T(8,128)(2,1)S(1)}, u32[]{:S(2)}, u32[]{:S(2)}) collective-permute-start(bf16[16,2048]{1,0:T(8,128)(2,1)S(1)} %pad_maximum_fusion.2), channel_id=1, source_target_pairs={{0,4},{1,5},{2,6},{3,7},{4,0},{5,1},{6,2},{7,3},{8,12},{9,13},{10,... | collective-permute-start | bytes 196616 | tf_op jit(solution)/shard_map/ppermute | solution.py:283
  19.4 2.9 %collective-permute-done.1 = bf16[16,2048]{1,0:T(8,128)(2,1)S(1)} collective-permute-done((bf16[16,2048]{1,0:T(8,128)(2,1)S(1)}, bf16[16,2048]{1,0:T(8,128)(2,1)S(1)}, u32[]{:S(2)}, u32[]{:S(2)}) %collective-permute-start.1) | collective-permute-done | bytes 65568 | tf_op jit(solution)/shard_map/ppermute | solution.py:283
  22.3 0.8 %pad_maximum_fusion.1 = bf16[32,2048]{1,0:T(8,128)(2,1)S(1)} fusion(bf16[16,2048]{1,0:T(8,128)(2,1)S(1)} %collective-permute-done.1, bf16[8,2048]{1,0:T(8,128)(2,1)S(1)} %collective-permute-done, bf16[8,2048]{1,0:T(8,128)(2,1)} %get-tuple-element.13), kind=kLoop, calls=%fused_computation.6 | loop fusion | flops 393216 | bytes 262144 | tf_op jit(solution)/shard_map/concatenate | solution.py:286
  23.0 1.6 %collective-permute-start.2 = (bf16[32,2048]{1,0:T(8,128)(2,1)S(1)}, bf16[32,2048]{1,0:T(8,128)(2,1)S(1)}, u32[]{:S(2)}, u32[]{:S(2)}) collective-permute-start(bf16[32,2048]{1,0:T(8,128)(2,1)S(1)} %pad_maximum_fusion.1), channel_id=1, source_target_pairs={{0,2},{1,3},{2,0},{3,1},{4,6},{5,7},{6,4},{7,5},{8,10},{9,11},{10,... | collective-permute-start | bytes 393224 | tf_op jit(solution)/shard_map/ppermute | solution.py:283
  24.6 0.0 collective-permute-done.4
  24.6 1.1 %convert_add_fusion = f32[64,2048]{1,0:T(8,128)S(1)} fusion(f32[64,2048]{1,0:T(8,128)} %get-tuple-element.20, bf16[64,2048]{1,0:T(8,128)(2,1)S(1)} %collective-permute-done.4), kind=kLoop, calls=%fused_computation | loop fusion | flops 262144 | bytes 1310720 | tf_op jit(solution)/shard_map/add | solution.py:288
  25.8 0.6 %collective-permute-start.5 = (bf16[32,2048]{1,0:T(8,128)(2,1)S(1)}, bf16[32,2048]{1,0:T(8,128)(2,1)S(1)}, u32[]{:S(2)}, u32[]{:S(2)}) collective-permute-start(bf16[32,2048]{1,0:T(8,128)(2,1)S(1)} %slice.39), channel_id=1, source_target_pairs={{0,2},{1,3},{2,0},{3,1},{4,6},{5,7},{6,4},{7,5},{8,10},{9,11},{10,... | collective-permute-start | bytes 393224 | tf_op jit(solution)/shard_map/ppermute | solution.py:283
  26.3 4.6 %collective-permute-done.5 = bf16[32,2048]{1,0:T(8,128)(2,1)S(1)} collective-permute-done((bf16[32,2048]{1,0:T(8,128)(2,1)S(1)}, bf16[32,2048]{1,0:T(8,128)(2,1)S(1)}, u32[]{:S(2)}, u32[]{:S(2)}) %collective-permute-start.5) | collective-permute-done | bytes 131104 | tf_op jit(solution)/shard_map/ppermute | solution.py:283
  31.0 1.6 %collective-permute-start.6 = (bf16[16,2048]{1,0:T(8,128)(2,1)S(1)}, bf16[16,2048]{1,0:T(8,128)(2,1)S(1)}, u32[]{:S(2)}, u32[]{:S(2)}) collective-permute-start(bf16[16,2048]{1,0:T(8,128)(2,1)S(1)} %slice.40), channel_id=1, source_target_pairs={{0,4},{1,5},{2,6},{3,7},{4,0},{5,1},{6,2},{7,3},{8,12},{9,13},{10,... | collective-permute-start | bytes 196616 | tf_op jit(solution)/shard_map/ppermute | solution.py:283
  32.7 0.0 collective-permute-done.2
  32.7 0.0 copy-done.1
  32.7 0.1 collective-permute-start.3
  32.8 2.6 %collective-permute-done.6 = bf16[16,2048]{1,0:T(8,128)(2,1)S(1)} collective-permute-done((bf16[16,2048]{1,0:T(8,128)(2,1)S(1)}, bf16[16,2048]{1,0:T(8,128)(2,1)S(1)}, u32[]{:S(2)}, u32[]{:S(2)}) %collective-permute-start.6) | collective-permute-done | bytes 65568 | tf_op jit(solution)/shard_map/ppermute | solution.py:283
  35.4 0.4 collective-permute-start.7
  35.8 4.5 %collective-permute-done.7 = bf16[8,2048]{1,0:T(8,128)(2,1)S(1)} collective-permute-done((bf16[8,2048]{1,0:T(8,128)(2,1)S(1)}, bf16[8,2048]{1,0:T(8,128)(2,1)S(1)}, u32[]{:S(2)}, u32[]{:S(2)}) %collective-permute-start.7) | collective-permute-done | bytes 32800 | tf_op jit(solution)/shard_map/ppermute | solution.py:283
  40.3 0.6 %slice_add_fusion.2.gr_ref = f32[8,2048]{1,0:T(8,128)} fusion(f32[16,2048]{1,0:T(8,128)S(1)} %slice_add_fusion.1, bf16[8,2048]{1,0:T(8,128)(2,1)S(1)} %collective-permute-done.7), kind=kLoop, calls=%fused_computation.8 | loop fusion | flops 32768 | bytes 163840 | tf_op jit(solution)/shard_map/add | solution.py:291
  40.9 0.0 collective-permute-done.3
  40.9 0.0 copy-start
  40.9 0.8 %copy-done = bf16[128,2048]{1,0:T(8,128)(2,1)} copy-done((bf16[128,2048]{1,0:T(8,128)(2,1)}, bf16[128,2048]{1,0:T(8,128)(2,1)S(1)}, u32[]{:S(2)}) %copy-start) | copy-done | bytes 524312
  41.7 5.1 %pair.1 = (bf16[8,128,128]{2,1,0:T(8,128)(2,1)}, f32[512,128]{1,0:T(8,128)}) custom-call(bf16[128,2048]{1,0:T(8,128)(2,1)} %copy-done, bf16[2048,1024]{1,0:T(8,128)(2,1)} %get-tuple-element.15.lp_ref, bf16[512,2048]{1,0:T(8,128)(2,1)} %outer_grad.1.got_ref, f32[1,128]{1,0:T(1,128)} %bitcast.12, s32[1,64]{1,0:T(1,128)} %bitcast.10, s32[1,128]{1,0:T(1,128)} %bitcast.7, ...), custom_call_target="tpu_custom_call" | custom-call | tf_op jit(solution)/shard_map/pair/pallas_call | solution.py:293
  46.9 2.6 %final.1 = bf16[64,8,256]{2,1,0:T(8,128)(2,1)} custom-call(f32[512,128]{1,0:T(8,128)} %get-tuple-element.19.gl_ref, f32[8,2048]{1,0:T(8,128)} %slice_add_fusion.2.gr_ref, f32[512,256]{1,0:T(8,128)} %get-tuple-element.22.scaled_ref, f32[512,128]{1,0:T(8,128)} %get-tuple-element.23.inv_ref, bf16[64,256]{1,0:T(8,128)(2,1)} %bitcast.5, s32[1,64]{1,0:T(1,128)} %bitcast.11, ...), custom_call_target="tpu_custom_call" | custom-call | tf_op jit(solution)/shard_map/final/pallas_call | solution.py:302
  (10 shorter events, 0.1 us)
Async XLA Ops:
  3.1 29.6 %copy-start.1 = (bf16[8,2048]{1,0:T(8,128)(2,1)S(1)}, bf16[8,2048]{1,0:T(8,128)(2,1)}, u32[]{:S(2)}) copy-start(bf16[8,2048]{1,0:T(8,128)(2,1)} %get-tuple-element.13) | copy-start | bytes 98308
  3.1 13.9 %collective-permute-start = (bf16[8,2048]{1,0:T(8,128)(2,1)}, bf16[8,2048]{1,0:T(8,128)(2,1)S(1)}, u32[]{:S(2)}, u32[]{:S(2)}) collective-permute-start(bf16[8,2048]{1,0:T(8,128)(2,1)} %get-tuple-element.13), channel_id=1, source_target_pairs={{0,8},{1,9},{2,10},{3,11},{4,12},{5,13},{6,14},{7,15},{8,0},{9,1},... | collective-permute-start | bytes 98312 | tf_op jit(solution)/shard_map/ppermute | solution.py:283
  13.1 11.5 %collective-permute-start.4 = (bf16[64,2048]{1,0:T(8,128)(2,1)}, bf16[64,2048]{1,0:T(8,128)(2,1)S(1)}, u32[]{:S(2)}, u32[]{:S(2)}) collective-permute-start(bf16[64,2048]{1,0:T(8,128)(2,1)} %get-tuple-element.21), channel_id=1, source_target_pairs={{0,1},{1,0},{2,3},{3,2},{4,5},{5,4},{6,7},{7,6},{8,9},{9,8},{10,11... | collective-permute-start | bytes 786440 | tf_op jit(solution)/shard_map/ppermute | solution.py:283
  17.8 4.5 %collective-permute-start.1 = (bf16[16,2048]{1,0:T(8,128)(2,1)S(1)}, bf16[16,2048]{1,0:T(8,128)(2,1)S(1)}, u32[]{:S(2)}, u32[]{:S(2)}) collective-permute-start(bf16[16,2048]{1,0:T(8,128)(2,1)S(1)} %pad_maximum_fusion.2), channel_id=1, source_target_pairs={{0,4},{1,5},{2,6},{3,7},{4,0},{5,1},{6,2},{7,3},{8,12},{9,13},{10,... | collective-permute-start | bytes 196616 | tf_op jit(solution)/shard_map/ppermute | solution.py:283
  23.0 9.6 %collective-permute-start.2 = (bf16[32,2048]{1,0:T(8,128)(2,1)S(1)}, bf16[32,2048]{1,0:T(8,128)(2,1)S(1)}, u32[]{:S(2)}, u32[]{:S(2)}) collective-permute-start(bf16[32,2048]{1,0:T(8,128)(2,1)S(1)} %pad_maximum_fusion.1), channel_id=1, source_target_pairs={{0,2},{1,3},{2,0},{3,1},{4,6},{5,7},{6,4},{7,5},{8,10},{9,11},{10,... | collective-permute-start | bytes 393224 | tf_op jit(solution)/shard_map/ppermute | solution.py:283
  25.8 5.2 %collective-permute-start.5 = (bf16[32,2048]{1,0:T(8,128)(2,1)S(1)}, bf16[32,2048]{1,0:T(8,128)(2,1)S(1)}, u32[]{:S(2)}, u32[]{:S(2)}) collective-permute-start(bf16[32,2048]{1,0:T(8,128)(2,1)S(1)} %slice.39), channel_id=1, source_target_pairs={{0,2},{1,3},{2,0},{3,1},{4,6},{5,7},{6,4},{7,5},{8,10},{9,11},{10,... | collective-permute-start | bytes 393224 | tf_op jit(solution)/shard_map/ppermute | solution.py:283
  31.0 4.3 %collective-permute-start.6 = (bf16[16,2048]{1,0:T(8,128)(2,1)S(1)}, bf16[16,2048]{1,0:T(8,128)(2,1)S(1)}, u32[]{:S(2)}, u32[]{:S(2)}) collective-permute-start(bf16[16,2048]{1,0:T(8,128)(2,1)S(1)} %slice.40), channel_id=1, source_target_pairs={{0,4},{1,5},{2,6},{3,7},{4,0},{5,1},{6,2},{7,3},{8,12},{9,13},{10,... | collective-permute-start | bytes 196616 | tf_op jit(solution)/shard_map/ppermute | solution.py:283
  32.7 8.2 %collective-permute-start.3 = (bf16[64,2048]{1,0:T(8,128)(2,1)S(1)}, bf16[64,2048]{1,0:T(8,128)(2,1)S(1)}, u32[]{:S(2)}, u32[]{:S(2)}) collective-permute-start(bf16[64,2048]{1,0:T(8,128)(2,1)S(1)} %pad_maximum_fusion), channel_id=1, source_target_pairs={{0,1},{1,0},{2,3},{3,2},{4,5},{5,4},{6,7},{7,6},{8,9},{9,8},{10,11... | collective-permute-start | bytes 786440 | tf_op jit(solution)/shard_map/ppermute | solution.py:283
  35.4 4.9 %collective-permute-start.7 = (bf16[8,2048]{1,0:T(8,128)(2,1)S(1)}, bf16[8,2048]{1,0:T(8,128)(2,1)S(1)}, u32[]{:S(2)}, u32[]{:S(2)}) collective-permute-start(bf16[8,2048]{1,0:T(8,128)(2,1)S(1)} %slice.41), channel_id=1, source_target_pairs={{0,8},{1,9},{2,10},{3,11},{4,12},{5,13},{6,14},{7,15},{8,0},{9,1},... | collective-permute-start | bytes 98312 | tf_op jit(solution)/shard_map/ppermute | solution.py:283
  40.9 0.8 %copy-start = (bf16[128,2048]{1,0:T(8,128)(2,1)}, bf16[128,2048]{1,0:T(8,128)(2,1)S(1)}, u32[]{:S(2)}) copy-start(bf16[128,2048]{1,0:T(8,128)(2,1)S(1)} %constant_dynamic-update-slice_fusion.r_ref) | copy-start | bytes 1572868

commit v2 on v1

--- a/solution.py
+++ b/solution.py
@@ -220,6 +220,7 @@
     return jax.ShapeDtypeStruct(dims, dtype)
 
 
+PARAMS = pltpu.CompilerParams(vmem_limit_bytes=16 * 1024 * 1024)
 VM = pl.BlockSpec(memory_space=pltpu.VMEM)
 SM = pl.BlockSpec(memory_space=pltpu.SMEM)
 
@@ -252,6 +253,7 @@
             pltpu.VMEM((seqs * local, LANES), F32),
             pltpu.VMEM((local * half, LANES), F32),
         ],
+        compiler_params=PARAMS,
         name="project",
     )(acts, proj_t, seq_row, res_mask)
 
@@ -267,6 +269,7 @@
         in_specs=[VM] * 3,
         out_specs=(VM,) * 5,
         scratch_shapes=[pltpu.VMEM(out_w.shape, F32), pltpu.VMEM(cot.shape, F32)],
+        compiler_params=PARAMS,
         name="pull",
     )(left, out_w, cot)
 
@@ -276,6 +279,7 @@
         in_specs=[VM, VM, VM, VM, SM],
         out_specs=VM,
         scratch_shapes=[pltpu.VMEM((total, LANES), F32), pltpu.VMEM((total, LANES), F32)],
+        compiler_params=PARAMS,
         name="outer_grad",
     )(wd, grel, seq_row, res_row, res_mask)
 
@@ -296,6 +300,7 @@
         in_specs=[VM, VM, VM, VM, VM, VM, SM],
         out_specs=(VM, VM),
         scratch_shapes=[pltpu.VMEM((total, 2 * pair), F32)],
+        compiler_params=PARAMS,
         name="pair",
     )(r, lp, got, out_b.reshape(1, pair), seq_row, res_row, res_mask)
 
@@ -309,6 +314,7 @@
             pltpu.VMEM((2 * chans, local * seqs), BF16),
             pltpu.VMEM((width // LANES, seqs * local, LANES), F32),
         ],
+        compiler_params=PARAMS,
         name="final",
     )(gl, right, scaled, inv, proj_t, seq_row, res_mask)
     return pair_out, grad

time: 49.9 us -> 43.2 us (0.87)
  Pallas kernels: 19.3 us -> 9.93 us
  local copies, waits for them, and re-layouts: 1.61 us -> 6.31 us
  other arithmetic: 3.32 us -> 0.14 us
  waiting for transfers between devices: 14.6 us -> 15.6 us
    unnamed x8 -> x28, local copies, waits for them, and re-layouts: 1.56 us -> 6.25 us
    pallas_call x1, Pallas kernels: 5.96 us -> 2.92 us  [body(): pl.pallas_call(functools.partial(pull_kernel, order), out_shape=(shape((f...]
    pallas_call x1, Pallas kernels: 5.14 us -> 2.62 us  [body(): pl.pallas_call(functools.partial(pair_kernel, order), out_shape=(shape((l...]
    pallas_call x1, Pallas kernels: 3.14 us -> 1.3 us  [body(): pl.pallas_call(functools.partial(outer_grad_kernel, order), out_shape=sha...]
    concatenate x3, other arithmetic: 1.55 us -> 0.03 us  [body(): r = jnp.concatenate([r, swap(r, b)], axis=0)]
    pallas_call x1, Pallas kernels: 2.45 us -> 1.17 us  [body(): pl.pallas_call(project_kernel, out_shape=(shape((local, flat), BF16), sha...]
    add x1, other arithmetic: 1.09 us -> 0.06 us  [body(): right = keep + swap(send, masks[0]).astype(F32)]
    ppermute x8, waiting for transfers between devices: 14.6 us -> 15.6 us  [swap(): return lax.ppermute(v, 'res', [(i, i ^ b) for i in range(size)])]
  transfers between devices with their start and end apart: 8 -> 8, of which waited for: 4 -> 4; matrix products, arithmetic and copies ran while one was open for 8% -> 0% of each run, Pallas kernels for 18% -> 10%
where the time goes in v2:
time: 43.2 us; the launch traced here: 42.9 us
  waiting for transfers between devices  15.6 us (36%)
  starting transfers between devices  10.1 us (23%)
  Pallas kernels  9.93 us (23%)
  local copies, waits for them, and re-layouts  6.31 us (15%)
  between operations  0.82 us (2%)
    ppermute x8, waiting for transfers between devices, swap(): return lax.ppermute(v, 'res', [(i, i ^ b) for i in range(size)])  15.6 us
    ppermute x8, starting transfers between devices, swap(): return lax.ppermute(v, 'res', [(i, i ^ b) for i in range(size)])  10.1 us
    unnamed x28, local copies, waits for them, and re-layouts  6.25 us
    pallas_call x1, Pallas kernels, body(): pl.pallas_call(functools.partial(pull_kernel, order), out_shape=(shape((f...  2.92 us
    pallas_call x1, Pallas kernels, body(): pl.pallas_call(functools.partial(pair_kernel, order), out_shape=(shape((l...  2.62 us
    pallas_call x1, Pallas kernels, body(): pl.pallas_call(final_kernel, out_shape=shape(acts.shape, BF16), in_specs=...  1.91 us
    pallas_call x1, Pallas kernels, body(): pl.pallas_call(functools.partial(outer_grad_kernel, order), out_shape=sha...  1.3 us
    pallas_call x1, Pallas kernels, body(): pl.pallas_call(project_kernel, out_shape=(shape((local, flat), BF16), sha...  1.17 us
  transfers between devices with their start and end apart: 8, of which 4 were waited for; matrix products, arithmetic and copies ran while one was open for 0% of the time, Pallas kernels for 10%

profile of v2, /device:TPU:0, one launch (start us, length us, event | category | flops | bytes accessed | tf_op | source)
XLA Modules:
  0.0 42.9 jit_solution(2707535588248038845)
XLA Ops:
  0.6 0.0 copy-start
  0.6 0.9 %copy-done = bf16[64,8,256]{2,1,0:T(8,128)(2,1)S(1)} copy-done((bf16[64,8,256]{2,1,0:T(8,128)(2,1)S(1)}, bf16[64,8,256]{2,1,0:T(8,128)(2,1)}, u32[]{:S(2)}) %copy-start) | copy-done | bytes 262168
  1.6 0.0 copy-start.3
  1.6 0.8 %copy-done.3 = bf16[256,64]{0,1:T(8,128)(2,1)S(1)} copy-done((bf16[256,64]{0,1:T(8,128)(2,1)S(1)}, bf16[256,64]{0,1:T(8,128)(2,1)}, u32[]{:S(2)}) %copy-start.3) | copy-done | bytes 32792
  2.3 0.0 copy-start.5
  2.3 0.7 %copy-done.5 = s32[128]{0:T(128)S(1)} copy-done((s32[128]{0:T(128)S(1)}, s32[128]{0:T(128)}, u32[]{:S(2)}) %copy-start.5) | copy-done | bytes 536
  3.0 0.0 copy-start.8
  3.0 0.7 %copy-done.8 = s32[64]{0:T(128)S(1)} copy-done((s32[64]{0:T(128)S(1)}, s32[64]{0:T(128)}, u32[]{:S(2)}) %copy-start.8) | copy-done | bytes 280
  3.7 0.0 copy-start.7
  3.7 0.0 copy-start.10
  3.7 0.0 copy-start.11
  3.7 1.2 %project.1 = (bf16[8,2048]{1,0:T(8,128)(2,1)S(1)}, bf16[512,32]{1,0:T(8,128)(2,1)S(1)}, f32[512,256]{1,0:T(8,128)S(1)}, f32[512,128]{1,0:T(8,128)S(1)}) custom-call(bf16[64,8,256]{2,1,0:T(8,128)(2,1)S(1)} %copy-done, bf16[64,256]{1,0:T(8,128)(2,1)S(1)} %bitcast.4, s32[1,64]{1,0:T(1,128)S(1)} %bitcast.8, s32[128]{0:T(128)S(1)} %copy-done.5), custom_call_target="tpu_custom_call" | custom-call | tf_op jit(solution)/shard_map/project/pallas_call | solution.py:241
  4.8 4.1 %collective-permute-start = (bf16[8,2048]{1,0:T(8,128)(2,1)S(1)}, bf16[8,2048]{1,0:T(8,128)(2,1)S(1)}, u32[]{:S(2)}, u32[]{:S(2)}) collective-permute-start(bf16[8,2048]{1,0:T(8,128)(2,1)S(1)} %get-tuple-element.13), channel_id=1, source_target_pairs={{0,8},{1,9},{2,10},{3,11},{4,12},{5,13},{6,14},{7,15},{8,0},{9,1},... | collective-permute-start | bytes 98312 | tf_op jit(solution)/shard_map/ppermute | solution.py:287
  9.0 0.0 copy-start.1
  9.0 0.9 %copy-done.1 = bf16[1024,128]{1,0:T(8,128)(2,1)S(1)} copy-done((bf16[1024,128]{1,0:T(8,128)(2,1)S(1)}, bf16[1024,128]{1,0:T(8,128)(2,1)}, u32[]{:S(2)}) %copy-start.1) | copy-done | bytes 262168
  9.9 0.0 copy-start.2
  9.9 0.9 %copy-done.2 = bf16[8,128,128]{2,1,0:T(8,128)(2,1)S(1)} copy-done((bf16[8,128,128]{2,1,0:T(8,128)(2,1)S(1)}, bf16[8,128,128]{2,1,0:T(8,128)(2,1)}, u32[]{:S(2)}) %copy-start.2) | copy-done | bytes 262168
  10.9 2.9 %pull.1 = (bf16[2048,1024]{1,0:T(8,128)(2,1)S(1)}, f32[64,2048]{1,0:T(8,128)S(1)}, bf16[64,2048]{1,0:T(8,128)(2,1)S(1)}, bf16[128,1024]{1,0:T(8,128)(2,1)S(1)}, bf16[1024,128]{1,0:T(8,128)(2,1)S(1)}) custom-call(bf16[512,32]{1,0:T(8,128)(2,1)S(1)} %get-tuple-element.14.left_ref, bf16[1024,128]{1,0:T(8,128)(2,1)S(1)} %copy-done.1, ...), custom_call_target="tpu_custom_call" | custom-call | tf_op jit(solution)/shard_map/pull/pallas_call | solution.py:260
  13.8 0.1 collective-permute-start.4
  13.9 0.0 copy-start.6
  13.9 0.6 %copy-done.6 = s32[128]{0:T(128)S(1)} copy-done((s32[128]{0:T(128)S(1)}, s32[128]{0:T(128)}, u32[]{:S(2)}) %copy-start.6) | copy-done | bytes 536
  14.5 0.0 copy-start.9
  14.5 0.7 %copy-done.9 = s32[64]{0:T(128)S(1)} copy-done((s32[64]{0:T(128)S(1)}, s32[64]{0:T(128)}, u32[]{:S(2)}) %copy-start.9) | copy-done | bytes 280
  15.2 1.3 %outer_grad.1.got_ref = bf16[512,2048]{1,0:T(8,128)(2,1)S(1)} custom-call(bf16[1024,128]{1,0:T(8,128)(2,1)S(1)} %get-tuple-element.16.wd_ref, bf16[128,1024]{1,0:T(8,128)(2,1)S(1)} %get-tuple-element.17.grel_ref, s32[1,64]{1,0:T(1,128)S(1)} %bitcast.9, s32[1,128]{1,0:T(1,128)S(1)} %bitcast.6, s32[128]{0:T(128)S(1)} %copy-done.6), custom_call_target="tpu_custom_call" | custom-call | tf_op jit(solution)/shard_map/outer_grad/pallas_call | solution.py:276
  16.5 0.0 collective-permute-done
  16.5 1.6 %collective-permute-start.1 = (bf16[16,2048]{1,0:T(8,128)(2,1)S(1)}, bf16[16,2048]{1,0:T(8,128)(2,1)S(1)}, u32[]{:S(2)}, u32[]{:S(2)}) collective-permute-start(bf16[16,2048]{1,0:T(8,128)(2,1)S(1)} %pad_maximum_fusion.2), channel_id=1, source_target_pairs={{0,4},{1,5},{2,6},{3,7},{4,0},{5,1},{6,2},{7,3},{8,12},{9,13},{10,... | collective-permute-start | bytes 196616 | tf_op jit(solution)/shard_map/ppermute | solution.py:287
  18.2 2.9 %collective-permute-done.1 = bf16[16,2048]{1,0:T(8,128)(2,1)S(1)} collective-permute-done((bf16[16,2048]{1,0:T(8,128)(2,1)S(1)}, bf16[16,2048]{1,0:T(8,128)(2,1)S(1)}, u32[]{:S(2)}, u32[]{:S(2)}) %collective-permute-start.1) | collective-permute-done | bytes 65568 | tf_op jit(solution)/shard_map/ppermute | solution.py:287
  21.1 1.6 %collective-permute-start.2 = (bf16[32,2048]{1,0:T(8,128)(2,1)S(1)}, bf16[32,2048]{1,0:T(8,128)(2,1)S(1)}, u32[]{:S(2)}, u32[]{:S(2)}) collective-permute-start(bf16[32,2048]{1,0:T(8,128)(2,1)S(1)} %pad_maximum_fusion.1), channel_id=1, source_target_pairs={{0,2},{1,3},{2,0},{3,1},{4,6},{5,7},{6,4},{7,5},{8,10},{9,11},{10,... | collective-permute-start | bytes 393224 | tf_op jit(solution)/shard_map/ppermute | solution.py:287
  22.7 0.0 collective-permute-done.4
  22.7 0.1 convert_add_fusion
  22.8 0.6 %collective-permute-start.5 = (bf16[32,2048]{1,0:T(8,128)(2,1)S(1)}, bf16[32,2048]{1,0:T(8,128)(2,1)S(1)}, u32[]{:S(2)}, u32[]{:S(2)}) collective-permute-start(bf16[32,2048]{1,0:T(8,128)(2,1)S(1)} %slice.39), channel_id=1, source_target_pairs={{0,2},{1,3},{2,0},{3,1},{4,6},{5,7},{6,4},{7,5},{8,10},{9,11},{10,... | collective-permute-start | bytes 393224 | tf_op jit(solution)/shard_map/ppermute | solution.py:287
  23.4 5.6 %collective-permute-done.5 = bf16[32,2048]{1,0:T(8,128)(2,1)S(1)} collective-permute-done((bf16[32,2048]{1,0:T(8,128)(2,1)S(1)}, bf16[32,2048]{1,0:T(8,128)(2,1)S(1)}, u32[]{:S(2)}, u32[]{:S(2)}) %collective-permute-start.5) | collective-permute-done | bytes 131104 | tf_op jit(solution)/shard_map/ppermute | solution.py:287
  29.0 1.6 %collective-permute-start.6 = (bf16[16,2048]{1,0:T(8,128)(2,1)S(1)}, bf16[16,2048]{1,0:T(8,128)(2,1)S(1)}, u32[]{:S(2)}, u32[]{:S(2)}) collective-permute-start(bf16[16,2048]{1,0:T(8,128)(2,1)S(1)} %slice.40), channel_id=1, source_target_pairs={{0,4},{1,5},{2,6},{3,7},{4,0},{5,1},{6,2},{7,3},{8,12},{9,13},{10,... | collective-permute-start | bytes 196616 | tf_op jit(solution)/shard_map/ppermute | solution.py:287
  30.7 0.0 collective-permute-done.2
  30.7 0.0 copy-start.4
  30.7 0.1 collective-permute-start.3
  30.8 2.6 %collective-permute-done.6 = bf16[16,2048]{1,0:T(8,128)(2,1)S(1)} collective-permute-done((bf16[16,2048]{1,0:T(8,128)(2,1)S(1)}, bf16[16,2048]{1,0:T(8,128)(2,1)S(1)}, u32[]{:S(2)}, u32[]{:S(2)}) %collective-permute-start.6) | collective-permute-done | bytes 65568 | tf_op jit(solution)/shard_map/ppermute | solution.py:287
  33.4 0.4 collective-permute-start.7
  33.8 4.5 %collective-permute-done.7 = bf16[8,2048]{1,0:T(8,128)(2,1)S(1)} collective-permute-done((bf16[8,2048]{1,0:T(8,128)(2,1)S(1)}, bf16[8,2048]{1,0:T(8,128)(2,1)S(1)}, u32[]{:S(2)}, u32[]{:S(2)}) %collective-permute-start.7) | collective-permute-done | bytes 32800 | tf_op jit(solution)/shard_map/ppermute | solution.py:287
  38.3 0.0 collective-permute-done.3
  38.3 0.0 copy-done.7
  38.3 0.0 copy-done.10
  38.4 0.0 copy-done.11
  38.4 2.6 %pair.1 = (bf16[8,128,128]{2,1,0:T(8,128)(2,1)}, f32[512,128]{1,0:T(8,128)S(1)}) custom-call(bf16[128,2048]{1,0:T(8,128)(2,1)S(1)} %constant_dynamic-update-slice_fusion.r_ref, bf16[2048,1024]{1,0:T(8,128)(2,1)S(1)} %get-tuple-element.15.lp_ref, bf16[512,2048]{1,0:T(8,128)(2,1)S(1)} %outer_grad.1.got_ref, f32[1,128]{1,0:T(1,128)S(1)} %bitcast.12, ...), custom_call_target="tpu_custom_call" | custom-call | tf_op jit(solution)/shard_map/pair/pallas_call | solution.py:297
  41.0 0.0 copy-done.4
  41.0 1.9 %final.1 = bf16[64,8,256]{2,1,0:T(8,128)(2,1)} custom-call(f32[512,128]{1,0:T(8,128)S(1)} %get-tuple-element.19.gl_ref, f32[8,2048]{1,0:T(8,128)S(1)} %slice_add_fusion.2.gr_ref, f32[512,256]{1,0:T(8,128)S(1)} %get-tuple-element.22.scaled_ref, f32[512,128]{1,0:T(8,128)S(1)} %get-tuple-element.23.inv_ref, bf16[64,256]{1,0:T(8,128)(2,1)S(1)} %bitcast.5, ...), custom_call_target="tpu_custom_call" | custom-call | tf_op jit(solution)/shard_map/final/pallas_call | solution.py:307
  (14 shorter events, 0.2 us)
Async XLA Ops:
  0.6 1.0 %copy-start = (bf16[64,8,256]{2,1,0:T(8,128)(2,1)S(1)}, bf16[64,8,256]{2,1,0:T(8,128)(2,1)}, u32[]{:S(2)}) copy-start(bf16[64,8,256]{2,1,0:T(8,128)(2,1)} %x_ref.1) | copy-start | bytes 786436
  1.6 0.8 %copy-start.3 = (bf16[256,64]{0,1:T(8,128)(2,1)S(1)}, bf16[256,64]{0,1:T(8,128)(2,1)}, u32[]{:S(2)}) copy-start(bf16[256,64]{0,1:T(8,128)(2,1)} %param.8) | copy-start | bytes 98308
  2.3 0.7 %copy-start.5 = (s32[128]{0:T(128)S(1)}, s32[128]{0:T(128)}, u32[]{:S(2)}) copy-start(s32[128]{0:T(128)} %res_ref.3) | copy-start | bytes 1540
  3.0 0.7 %copy-start.8 = (s32[64]{0:T(128)S(1)}, s32[64]{0:T(128)}, u32[]{:S(2)}) copy-start(s32[64]{0:T(128)} %param.12) | copy-start | bytes 772
  3.7 34.7 %copy-start.7 = (s32[128]{0:T(128)S(1)}, s32[128]{0:T(128)}, u32[]{:S(2)}) copy-start(s32[128]{0:T(128)} %res_ref.3) | copy-start | bytes 1540
  3.7 34.7 %copy-start.10 = (s32[64]{0:T(128)S(1)}, s32[64]{0:T(128)}, u32[]{:S(2)}) copy-start(s32[64]{0:T(128)} %param.12) | copy-start | bytes 772
  3.7 34.7 %copy-start.11 = (f32[128]{0:T(128)S(1)}, f32[128]{0:T(128)}, u32[]{:S(2)}) copy-start(f32[128]{0:T(128)} %param.10) | copy-start | bytes 1540
  4.8 11.7 %collective-permute-start = (bf16[8,2048]{1,0:T(8,128)(2,1)S(1)}, bf16[8,2048]{1,0:T(8,128)(2,1)S(1)}, u32[]{:S(2)}, u32[]{:S(2)}) collective-permute-start(bf16[8,2048]{1,0:T(8,128)(2,1)S(1)} %get-tuple-element.13), channel_id=1, source_target_pairs={{0,8},{1,9},{2,10},{3,11},{4,12},{5,13},{6,14},{7,15},{8,0},{9,1},... | collective-permute-start | bytes 98312 | tf_op jit(solution)/shard_map/ppermute | solution.py:287
  9.0 0.9 %copy-start.1 = (bf16[1024,128]{1,0:T(8,128)(2,1)S(1)}, bf16[1024,128]{1,0:T(8,128)(2,1)}, u32[]{:S(2)}) copy-start(bf16[1024,128]{1,0:T(8,128)(2,1)} %wo_ref.1) | copy-start | bytes 786436
  9.9 0.9 %copy-start.2 = (bf16[8,128,128]{2,1,0:T(8,128)(2,1)S(1)}, bf16[8,128,128]{2,1,0:T(8,128)(2,1)}, u32[]{:S(2)}) copy-start(bf16[8,128,128]{2,1,0:T(8,128)(2,1)} %g_ref.1) | copy-start | bytes 786436
  13.8 8.9 %collective-permute-start.4 = (bf16[64,2048]{1,0:T(8,128)(2,1)S(1)}, bf16[64,2048]{1,0:T(8,128)(2,1)S(1)}, u32[]{:S(2)}, u32[]{:S(2)}) collective-permute-start(bf16[64,2048]{1,0:T(8,128)(2,1)S(1)} %get-tuple-element.21), channel_id=1, source_target_pairs={{0,1},{1,0},{2,3},{3,2},{4,5},{5,4},{6,7},{7,6},{8,9},{9,8},{10,11... | collective-permute-start | bytes 786440 | tf_op jit(solution)/shard_map/ppermute | solution.py:287
  13.9 0.7 %copy-start.6 = (s32[128]{0:T(128)S(1)}, s32[128]{0:T(128)}, u32[]{:S(2)}) copy-start(s32[128]{0:T(128)} %res_ref.3) | copy-start | bytes 1540
  14.5 0.7 %copy-start.9 = (s32[64]{0:T(128)S(1)}, s32[64]{0:T(128)}, u32[]{:S(2)}) copy-start(s32[64]{0:T(128)} %param.12) | copy-start | bytes 772
  16.5 4.5 %collective-permute-start.1 = (bf16[16,2048]{1,0:T(8,128)(2,1)S(1)}, bf16[16,2048]{1,0:T(8,128)(2,1)S(1)}, u32[]{:S(2)}, u32[]{:S(2)}) collective-permute-start(bf16[16,2048]{1,0:T(8,128)(2,1)S(1)} %pad_maximum_fusion.2), channel_id=1, source_target_pairs={{0,4},{1,5},{2,6},{3,7},{4,0},{5,1},{6,2},{7,3},{8,12},{9,13},{10,... | collective-permute-start | bytes 196616 | tf_op jit(solution)/shard_map/ppermute | solution.py:287
  21.1 9.6 %collective-permute-start.2 = (bf16[32,2048]{1,0:T(8,128)(2,1)S(1)}, bf16[32,2048]{1,0:T(8,128)(2,1)S(1)}, u32[]{:S(2)}, u32[]{:S(2)}) collective-permute-start(bf16[32,2048]{1,0:T(8,128)(2,1)S(1)} %pad_maximum_fusion.1), channel_id=1, source_target_pairs={{0,2},{1,3},{2,0},{3,1},{4,6},{5,7},{6,4},{7,5},{8,10},{9,11},{10,... | collective-permute-start | bytes 393224 | tf_op jit(solution)/shard_map/ppermute | solution.py:287
  22.8 6.2 %collective-permute-start.5 = (bf16[32,2048]{1,0:T(8,128)(2,1)S(1)}, bf16[32,2048]{1,0:T(8,128)(2,1)S(1)}, u32[]{:S(2)}, u32[]{:S(2)}) collective-permute-start(bf16[32,2048]{1,0:T(8,128)(2,1)S(1)} %slice.39), channel_id=1, source_target_pairs={{0,2},{1,3},{2,0},{3,1},{4,6},{5,7},{6,4},{7,5},{8,10},{9,11},{10,... | collective-permute-start | bytes 393224 | tf_op jit(solution)/shard_map/ppermute | solution.py:287
  29.0 4.3 %collective-permute-start.6 = (bf16[16,2048]{1,0:T(8,128)(2,1)S(1)}, bf16[16,2048]{1,0:T(8,128)(2,1)S(1)}, u32[]{:S(2)}, u32[]{:S(2)}) collective-permute-start(bf16[16,2048]{1,0:T(8,128)(2,1)S(1)} %slice.40), channel_id=1, source_target_pairs={{0,4},{1,5},{2,6},{3,7},{4,0},{5,1},{6,2},{7,3},{8,12},{9,13},{10,... | collective-permute-start | bytes 196616 | tf_op jit(solution)/shard_map/ppermute | solution.py:287
  30.7 10.3 %copy-start.4 = (bf16[256,64]{0,1:T(8,128)(2,1)S(1)}, bf16[256,64]{0,1:T(8,128)(2,1)}, u32[]{:S(2)}) copy-start(bf16[256,64]{0,1:T(8,128)(2,1)} %param.8) | copy-start | bytes 98308
  30.7 7.6 %collective-permute-start.3 = (bf16[64,2048]{1,0:T(8,128)(2,1)S(1)}, bf16[64,2048]{1,0:T(8,128)(2,1)S(1)}, u32[]{:S(2)}, u32[]{:S(2)}) collective-permute-start(bf16[64,2048]{1,0:T(8,128)(2,1)S(1)} %pad_maximum_fusion), channel_id=1, source_target_pairs={{0,1},{1,0},{2,3},{3,2},{4,5},{5,4},{6,7},{7,6},{8,9},{9,8},{10,11... | collective-permute-start | bytes 786440 | tf_op jit(solution)/shard_map/ppermute | solution.py:287
  33.4 4.9 %collective-permute-start.7 = (bf16[8,2048]{1,0:T(8,128)(2,1)S(1)}, bf16[8,2048]{1,0:T(8,128)(2,1)S(1)}, u32[]{:S(2)}, u32[]{:S(2)}) collective-permute-start(bf16[8,2048]{1,0:T(8,128)(2,1)S(1)} %slice.41), channel_id=1, source_target_pairs={{0,8},{1,9},{2,10},{3,11},{4,12},{5,13},{6,14},{7,15},{8,0},{9,1},... | collective-permute-start | bytes 98312 | tf_op jit(solution)/shard_map/ppermute | solution.py:287
